TPU v7x, 32 devices: a whole 2x2x4 slice. The times are simulated.
32 devices in a mesh: dp: 4 (over z), ctx: 8 (over y, x, core).
Axes of the slice: x: 2, y: 2, z: 4, core: 2. Of those that a mesh axis runs over, the one named last changes fastest.
Arguments:
- queries: bfloat16 [4, 1024, 1024], P('dp', 'ctx'), may hold values from -6 to 6
- keys: bfloat16 [4, 1024, 1024], P('dp', 'ctx'), may hold values from -6 to 6
- values: bfloat16 [4, 1024, 1024], P('dp', 'ctx'), may hold values from -6 to 6
- outputs: bfloat16 [4, 1024, 1024], P('dp', 'ctx'), may hold values from -1.25 to 1.25
- d_out: bfloat16 [4, 1024, 1024], P('dp', 'ctx'), may hold values from -6 to 6
- lse: float32 [4, 16, 1024], P('dp', None, 'ctx'), may hold values from 3 to 5
- glob_keys: bfloat16 [128, 1024], replicated, may hold values from -6 to 6
- glob_values: bfloat16 [128, 1024], replicated, may hold values from -6 to 6
- rand_owner: int32 [16, 3], P('ctx'), may hold values from 0 to 7, all different within a row; in each aligned block of 2 rows (0 to 1, 2 to 3, ...) at most 2 rows name the same one
- rand_local: int32 [16, 3], P('ctx'), may hold values from 0 to 1
Outputs:
- d_queries: bfloat16 [4, 1024, 1024], P('dp', 'ctx')
- d_keys: bfloat16 [4, 1024, 1024], P('dp', 'ctx')
- d_values: bfloat16 [4, 1024, 1024], P('dp', 'ctx')
- d_glob_keys: float32 [128, 1024], replicated
- d_glob_values: float32 [128, 1024], replicated
Inputs may be any that keep to these rules, and one draw needn't show every extreme that they name: `rand_owner`: the 3 random blocks of one query block lie on different ctx indices. Among the 2 query blocks of one device no ctx index is named more than 2 times.
All inputs are finite; a program needn't handle non-finite values.
Results may differ from a plain program's by a relative error of at most 0.0055.
Values may be sent and summed in bfloat16 or wider, within the bound.
A program may use at most 128 MiB of HBM per device.

v0:
```python
import jax
import jax.numpy as jnp
from jax import lax
from jax.sharding import PartitionSpec as P

HEADS = 16
HDIM = 64
BLK = 64
GLOB = 128


def extended(block, sides, width):
    for axis, dim in sides:
        count = lax.axis_size(axis)
        forward = [(i, i + 1) for i in range(count - 1)]
        forward.append((count - 1, 0))
        backward = [(target, source) for source, target in forward]
        low = lax.ppermute(
            lax.slice_in_dim(block, block.shape[dim] - width, None, axis=dim), axis, forward
        )
        high = lax.ppermute(lax.slice_in_dim(block, 0, width, axis=dim), axis, backward)
        block = jnp.concatenate([low, block, high], axis=dim)
    return block


def block_grads(query_blk, dout_blk, lse_blk, delta_blk, key_blk, value_blk):
    scaling = HDIM ** (-0.5)
    scores = (
        jnp.einsum("nqhe,nkhe->nhqk", query_blk, key_blk, preferred_element_type=jnp.float32)
        * scaling
    )
    probability = jnp.exp(scores - lse_blk[..., None])
    prob_low = probability.astype(jnp.bfloat16)
    d_probability = jnp.einsum(
        "nqhe,nkhe->nhqk", dout_blk, value_blk, preferred_element_type=jnp.float32
    )
    d_scores = (probability * (d_probability - delta_blk[..., None])).astype(jnp.bfloat16)
    grad_q = (
        jnp.einsum("nhqk,nkhe->nqhe", d_scores, key_blk, preferred_element_type=jnp.float32)
        * scaling
    )
    grad_k = (
        jnp.einsum("nhqk,nqhe->nkhe", d_scores, query_blk, preferred_element_type=jnp.float32)
        * scaling
    )
    grad_v = jnp.einsum("nhqk,nqhe->nkhe", prob_low, dout_blk, preferred_element_type=jnp.float32)
    return (grad_q, grad_k, grad_v)


def spread_window(section):
    pad_rest = ((0, 0), (0, 0), (0, 0))
    lower = jnp.pad(section[:, :BLK], ((0, 2),) + pad_rest)
    middle = jnp.pad(section[:, BLK : 2 * BLK], ((1, 1),) + pad_rest)
    upper = jnp.pad(section[:, 2 * BLK :], ((2, 0),) + pad_rest)
    return lower + middle + upper


def shards(
    queries, keys, values, outputs, d_out, lse, glob_keys, glob_values, rand_owner, rand_local
):
    tokens_dev = queries.shape[1]
    feature_dim = queries.shape[2]
    blocks = tokens_dev // BLK
    cycle_size = lax.axis_size("ctx")
    per_block = rand_owner.shape[1]
    pairs = blocks * per_block
    query_blk = queries.reshape(blocks, BLK, HEADS, HDIM)
    dout_blk = d_out.reshape(blocks, BLK, HEADS, HDIM)
    product = d_out.astype(jnp.float32) * outputs.astype(jnp.float32)
    delta_blk = jnp.sum(product.reshape(blocks, BLK, HEADS, HDIM), axis=3).transpose(0, 2, 1)
    lse_blk = lse.reshape(HEADS, blocks, BLK).transpose(1, 0, 2)
    key_value = jnp.stack([keys[0], values[0]])
    padded = extended(key_value, (("ctx", 1),), BLK)

    def split_blocks(section):
        return section.reshape(2, blocks, BLK, HEADS, HDIM)

    window = jnp.concatenate(
        [
            split_blocks(padded[:, :tokens_dev]),
            split_blocks(padded[:, BLK : BLK + tokens_dev]),
            split_blocks(padded[:, 2 * BLK :]),
        ],
        axis=2,
    )
    dq_win, dk_win, dv_win = block_grads(
        query_blk, dout_blk, lse_blk, delta_blk, window[0], window[1]
    )
    grad_grid = jnp.stack([spread_window(dk_win), spread_window(dv_win)]).reshape(
        2, tokens_dev + 2 * BLK, feature_dim
    )
    edge_rims = jnp.concatenate([grad_grid[:, :BLK], grad_grid[:, tokens_dev + BLK :]], axis=1)
    returned = extended(edge_rims, (("ctx", 1),), BLK)
    kv_grad = grad_grid[:, BLK : tokens_dev + BLK]
    kv_grad = kv_grad.at[:, :BLK].add(returned[:, :BLK])
    kv_grad = kv_grad.at[:, tokens_dev - BLK :].add(returned[:, 3 * BLK :])
    mem_keys = jnp.broadcast_to(
        glob_keys.reshape(1, GLOB, HEADS, HDIM), (blocks, GLOB, HEADS, HDIM)
    )
    mem_values = jnp.broadcast_to(
        glob_values.reshape(1, GLOB, HEADS, HDIM), (blocks, GLOB, HEADS, HDIM)
    )
    dq_mem, dk_mem, dv_mem = block_grads(
        query_blk, dout_blk, lse_blk, delta_blk, mem_keys, mem_values
    )
    mem_terms = jnp.stack([jnp.sum(dk_mem, axis=0), jnp.sum(dv_mem, axis=0)]).reshape(
        2, GLOB, feature_dim
    )
    memory_total = lax.psum(mem_terms, ("dp", "ctx"))
    capacity = min(blocks, max(2, 2 * blocks * per_block // cycle_size))
    owner_flat = rand_owner.reshape(-1)
    local_flat = rand_local.reshape(-1)
    owner_hits = (owner_flat[:, None] == jnp.arange(cycle_size, dtype=jnp.int32)[None, :]).astype(
        jnp.int32
    )
    earlier = jnp.cumsum(owner_hits, axis=0) - owner_hits
    slot_rank = jnp.sum(earlier * owner_hits, axis=1)
    slot_index = owner_flat * capacity + slot_rank
    wanted = (
        jnp.zeros((cycle_size * capacity,), jnp.int32)
        .at[slot_index]
        .set(local_flat)
        .reshape(cycle_size, capacity)
    )
    kv_blocks = jnp.stack(
        [keys[0].reshape(blocks, BLK, feature_dim), values[0].reshape(blocks, BLK, feature_dim)],
        axis=1,
    )
    query_pairs = jnp.repeat(query_blk, per_block, axis=0)
    dout_pairs = jnp.repeat(dout_blk, per_block, axis=0)
    lse_pairs = jnp.repeat(lse_blk, per_block, axis=0)
    delta_pairs = jnp.repeat(delta_blk, per_block, axis=0)
    slots_all = cycle_size * capacity
    asked_ids = lax.all_to_all(wanted, "ctx", split_axis=0, concat_axis=0, tiled=True)
    picked = kv_blocks[asked_ids]
    fetched, asked_ids = (
        lax.all_to_all(picked, "ctx", split_axis=0, concat_axis=0, tiled=True),
        asked_ids,
    )
    chosen = fetched.reshape(slots_all, 2, BLK, HEADS, HDIM)[slot_index]
    dq_pair, dk_pair, dv_pair = block_grads(
        query_pairs, dout_pairs, lse_pairs, delta_pairs, chosen[:, 0], chosen[:, 1]
    )
    dq_rand = lax.optimization_barrier(dq_pair.astype(jnp.bfloat16)).astype(jnp.float32)
    pair_grads = (
        jnp.stack([dk_pair, dv_pair], axis=1)
        .reshape(pairs, 2, BLK, feature_dim)
        .astype(jnp.bfloat16)
    )
    grad_slots = (
        jnp.zeros((slots_all, 2, BLK, feature_dim), jnp.bfloat16).at[slot_index].set(pair_grads)
    )
    arrived = lax.all_to_all(
        grad_slots.reshape(cycle_size, capacity, 2, BLK, feature_dim),
        "ctx",
        split_axis=0,
        concat_axis=0,
        tiled=True,
    )
    received = arrived.reshape(slots_all, 2, BLK, feature_dim)
    kv_rand = (
        jnp.zeros((blocks, 2, BLK, feature_dim), jnp.float32)
        .at[asked_ids.reshape(-1)]
        .add(received.astype(jnp.float32))
    )
    dq_rand_sum = jnp.sum(dq_rand.reshape(blocks, per_block, BLK, HEADS, HDIM), axis=1)
    grad_queries = (
        (dq_win + dq_mem + dq_rand_sum).reshape(1, tokens_dev, feature_dim).astype(jnp.bfloat16)
    )
    grad_keys = (
        (kv_grad[0] + kv_rand[:, 0].reshape(tokens_dev, feature_dim))
        .reshape(1, tokens_dev, feature_dim)
        .astype(jnp.bfloat16)
    )
    grad_values = (
        (kv_grad[1] + kv_rand[:, 1].reshape(tokens_dev, feature_dim))
        .reshape(1, tokens_dev, feature_dim)
        .astype(jnp.bfloat16)
    )
    return (grad_queries, grad_keys, grad_values, memory_total[0], memory_total[1])


def solution(mesh):
    return jax.shard_map(
        shards,
        mesh=mesh,
        in_specs=(
            P("dp", "ctx", None),
            P("dp", "ctx", None),
            P("dp", "ctx", None),
            P("dp", "ctx", None),
            P("dp", "ctx", None),
            P("dp", None, "ctx"),
            P(),
            P(),
            P("ctx", None),
            P("ctx", None),
        ),
        out_specs=(P("dp", "ctx", None), P("dp", "ctx", None), P("dp", "ctx", None), P(), P()),
        check_vma=False,
    )
```

profile of v0, /device:TPU:0, one launch (start us, length us, event | category | flops | bytes accessed | tf_op | source)
XLA Modules:
  0.0 246.8 jit_solution(17565777443147992249)
XLA Ops:
  11.0 5.2 %all-to-all-start = ((s32[8,1,2]{2,1,0:T(1,128)}), s32[8,1,2]{2,1,0:T(1,128)S(1)}, u32[]{:S(2)}, u32[]{:S(2)}) async-start(s32[8,1,2]{2,1,0:T(1,128)} %bitcast.12), calls=%async_computation | async-start | bytes 8192 | tf_op jit(solution)/shard_map/all_to_all | solution.py:134
  17.3 3.5 %all-to-all-done = s32[8,1,2]{2,1,0:T(1,128)S(1)} async-done(((s32[8,1,2]{2,1,0:T(1,128)}), s32[8,1,2]{2,1,0:T(1,128)S(1)}, u32[]{:S(2)}, u32[]{:S(2)}) %all-to-all-start) | async-done | bytes 96 | tf_op jit(solution)/shard_map/all_to_all | solution.py:134
  21.0 2.8 %gather_fusion = bf16[16,2,64,1024]{3,2,1,0:T(8,128)(2,1)} fusion(bf16[2,2,64,1024]{3,2,0,1:T(8,128)(2,1)S(1)} %pad_maximum_fusion.5, s32[1024]{0:T(1024)S(1)} %pad_clamp_fusion.1), kind=kCustom, calls=%fused_computation | custom fusion | bytes 8388672 | tf_op jit(solution)/shard_map/gather | solution.py:135
  23.8 4.7 %all-to-all-start.1 = ((bf16[8,2,2,64,1024]{4,3,2,1,0:T(8,128)(2,1)}), bf16[8,2,2,64,1024]{4,3,2,1,0:T(8,128)(2,1)}, u32[]{:S(2)}, u32[]{:S(2)}) async-start(bf16[8,2,2,64,1024]{4,3,2,1,0:T(8,128)(2,1)} %bitcast.105), calls=%async_computation.1 | async-start | bytes 8388608 | tf_op jit(solution)/shard_map/all_to_all | solution.py:137
  29.9 2.3 collective-permute-start.1
  42.5 2.0 copy.129
  45.7 39.9 %collective-permute-done = bf16[2,64,1024]{2,1,0:T(8,128)(2,1)} collective-permute-done((bf16[2,64,1024]{2,1,0:T(8,128)(2,1)}, bf16[2,64,1024]{2,1,0:T(8,128)(2,1)}, u32[]{:S(2)}, u32[]{:S(2)}) %collective-permute-start) | collective-permute-done | bytes 262176 | tf_op jit(solution)/shard_map/ppermute | solution.py:18
  87.5 2.5 %reshape.256 = bf16[2,2,64,16,64]{4,3,2,1,0:T(8,128)(2,1)} reshape(bf16[2,128,1024]{2,1,0:T(8,128)(2,1)} %get-tuple-element.66) | data formatting | bytes 1048576 | tf_op jit(solution)/shard_map/reshape | solution.py:76
  90.0 2.7 %copy.130 = bf16[2,2,64,16,64]{2,4,3,1,0:T(8,128)(2,1)} copy(bf16[2,2,64,16,64]{4,3,2,1,0:T(8,128)(2,1)} %reshape.256) | data formatting | bytes 1048576 | tf_op jit(solution)/shard_map/reshape | solution.py:76
  94.3 2.7 %copy.128 = bf16[2,2,64,16,64]{2,4,3,1,0:T(8,128)(2,1)} copy(bf16[2,2,64,16,64]{4,3,2,1,0:T(8,128)(2,1)} %reshape.254) | data formatting | bytes 1048576 | tf_op jit(solution)/shard_map/reshape | solution.py:76
  97.0 2.5 %pad_maximum_fusion = bf16[2,2,192,16,64]{2,4,3,1,0:T(8,128)(2,1)S(1)} fusion(bf16[2,2,64,16,64]{2,4,3,1,0:T(8,128)(2,1)} %copy.130, bf16[2,2,64,16,64]{2,4,3,1,0:T(8,128)(2,1)S(1)} %copy.129, bf16[2,2,64,16,64]{2,4,3,1,0:T(8,128)(2,1)} %copy.128), kind=kLoop, calls=%fused_computation.12 | loop fusion | flops 4718592 | bytes 3145728 | tf_op jit(solution)/shard_map/concatenate | solution.py:78
  104.3 11.6 %reshape.262 = bf16[16,2,64,16,64]{4,3,2,1,0:T(8,128)(2,1)} reshape(bf16[8,2,2,64,1024]{4,3,2,1,0:T(8,128)(2,1)} %all-to-all-done.1) | data formatting | bytes 8388608 | tf_op jit(solution)/shard_map/reshape | solution.py:140
  115.9 4.5 %gather_fusion.1 = bf16[6,2,64,16,64]{4,3,2,1,0:T(8,128)(2,1)S(1)} fusion(bf16[16,2,64,16,64]{4,3,2,1,0:T(8,128)(2,1)} %reshape.262, s32[1024]{0:T(1024)S(1)} %pad_clamp_fusion), kind=kCustom, calls=%fused_computation.1 | custom fusion | bytes 3145752 | tf_op jit(solution)/shard_map/gather | solution.py:140
  125.7 2.2 copy.156
  127.9 3.4 %stack.39 = bf16[6,1,64,1024]{3,2,0,1:T(8,128)(2,1)} reshape(bf16[6,64,16,64]{3,2,1,0:T(8,128)(2,1)} %copy.156) | data formatting | bytes 1572864 | tf_op jit(solution)/shard_map/stack | solution.py:146
  131.4 3.1 %multiply_convert_fusion.2 = bf16[6,16,64,64]{3,2,1,0:T(8,128)(2,1)S(1)} fusion(f32[6,16,64,64]{3,2,1,0:T(8,128)S(1)} %fusion.10, bf16[6,64,16,64]{3,1,2,0:T(8,128)(2,1)} %bitcast.109, bf16[6,1,64,16,64]{4,3,2,1,0:T(8,128)(2,1)} %get-tuple-element.49, f32[6,16,64]{2,1,0:T(8,128)S(1)} %bitcast.127, f32[6,16,64]{2,1,0:T(8,128)S(1)} %bitcast.121), kind=kOutput, calls=%fused_computation.9 | convolution fusion | flops 52297728 | bytes 3981312 | tf_op jit(solution)/shard_map/nqhe,nkhe->nhqk/dot_general | solution.py:34
  138.1 2.5 %broadcast_in_dim.51 = bf16[16,2,64,1024]{3,2,1,0:T(8,128)(2,1)} broadcast(bf16[]{:T(256)} %constant.82.clone.1), dimensions={} | broadcast | bytes 4194306 | tf_op jit(solution)/shard_map/broadcast_in_dim | solution.py:151
  140.6 4.8 %scatter_fusion = bf16[16,2,64,1024]{3,2,1,0:T(8,128)(2,1)} fusion(bf16[16,2,64,1024]{3,2,1,0:T(8,128)(2,1)} %broadcast_in_dim.51, s32[6]{0:T(128)S(1)} %fusion.34, bf16[6,2,64,1024]{3,2,1,0:T(8,128)(2,1)S(1)} %copy.157), kind=kCustom, calls=%fused_computation.3 | custom fusion | bytes 4718616 | tf_op jit(solution)/shard_map/scatter | solution.py:151
  145.4 5.0 %all-to-all-start.2 = ((bf16[8,2,2,64,1024]{4,3,2,1,0:T(8,128)(2,1)}), bf16[8,2,2,64,1024]{4,3,2,1,0:T(8,128)(2,1)}, u32[]{:S(2)}, u32[]{:S(2)}) async-start(bf16[8,2,2,64,1024]{4,3,2,1,0:T(8,128)(2,1)} %bitcast.104), calls=%async_computation.2 | async-start | bytes 8388608 | tf_op jit(solution)/shard_map/all_to_all | solution.py:153
  151.3 2.0 copy.152
  153.3 2.9 %stack.35 = f32[1,256,1024]{2,1,0:T(8,128)} reshape(f32[4,64,16,64]{3,2,1,0:T(8,128)} %copy.152) | data formatting | bytes 2097152 | tf_op jit(solution)/shard_map/stack | solution.py:89
  158.1 2.0 copy.154
  160.2 2.1 stack.36
  164.8 2.5 %collective-permute-start.3 = (f32[2,64,1024]{2,1,0:T(8,128)}, f32[2,64,1024]{2,1,0:T(8,128)}, u32[]{:S(2)}, u32[]{:S(2)}) collective-permute-start(f32[2,64,1024]{2,1,0:T(8,128)} %get-tuple-element.51), channel_id=1, source_target_pairs={{1,0},{2,1},{3,2},{4,3},{5,4},{6,5},{7,6},{0,7},{9,8},{10,9},{11,1... | collective-permute-start | bytes 1572872 | tf_op jit(solution)/shard_map/ppermute | solution.py:21
  168.8 10.2 %all-reduce.8.cloned.1.call-done = f32[2,128,1024]{1,2,0:T(8,128)} async-done(((f32[2,128,1024]{1,2,0:T(8,128)}), f32[2,128,1024]{1,2,0:T(8,128)}) %all-reduce.8.cloned.1.call-update) | async-done | bytes 1048592 | tf_op jit(solution)/shard_map/psum | solution.py:109
  179.0 2.1 slice_bitcast_fusion.5
  182.1 2.2 copy.161
  184.3 27.9 %collective-permute-done.2 = f32[2,64,1024]{2,1,0:T(8,128)} collective-permute-done((f32[2,64,1024]{2,1,0:T(8,128)}, f32[2,64,1024]{2,1,0:T(8,128)}, u32[]{:S(2)}, u32[]{:S(2)}) %collective-permute-start.2) | collective-permute-done | bytes 524320 | tf_op jit(solution)/shard_map/ppermute | solution.py:18
  212.2 2.1 fusion.27
  214.3 2.1 fusion.26
  220.4 6.5 %bitcast_convert_fusion = f32[16,2,64,1024]{3,2,1,0:T(8,128)} fusion(bf16[8,2,2,64,1024]{4,3,2,1,0:T(8,128)(2,1)} %all-to-all-done.2), kind=kLoop, calls=%fused_computation.5 | loop fusion | flops 2097152 | bytes 12582912 | tf_op jit(solution)/shard_map/convert_element_type | solution.py:164
  227.1 10.8 %scatter_fusion.1 = f32[2,2,64,1024]{3,2,1,0:T(8,128)S(1)} fusion(f32[2,2,64,1024]{3,2,1,0:T(8,128)S(1)} %broadcast_in_dim.50, s32[16]{0:T(128)S(1)} %fusion.35, f32[16,2,64,1024]{3,2,1,0:T(8,128)} %bitcast_convert_fusion), kind=kCustom, calls=%fused_computation.4 | custom fusion | flops 2097152 | bytes 25165888 | tf_op jit(solution)/shard_map/scatter-add | solution.py:164
  (148 shorter events, 48.9 us)
Async XLA Ops:
  11.0 9.8 %all-to-all-start = ((s32[8,1,2]{2,1,0:T(1,128)}), s32[8,1,2]{2,1,0:T(1,128)S(1)}, u32[]{:S(2)}, u32[]{:S(2)}) async-start(s32[8,1,2]{2,1,0:T(1,128)} %bitcast.12), calls=%async_computation | async-start | bytes 8192 | tf_op jit(solution)/shard_map/all_to_all | solution.py:134
  23.8 4.8 %copy-start.26 = (bf16[1,128,1024]{2,1,0:T(8,128)(2,1)S(1)}, bf16[1,128,1024]{2,1,0:T(8,128)(2,1)}, u32[]{:S(2)}) copy-start(bf16[1,128,1024]{2,1,0:T(8,128)(2,1)} %param.15) | copy-start | bytes 786436
  23.8 4.9 %copy-start.27 = (bf16[1,128,1024]{2,1,0:T(8,128)(2,1)S(1)}, bf16[1,128,1024]{2,1,0:T(8,128)(2,1)}, u32[]{:S(2)}) copy-start(bf16[1,128,1024]{2,1,0:T(8,128)(2,1)} %param.16) | copy-start | bytes 786436
  23.8 80.5 %all-to-all-start.1 = ((bf16[8,2,2,64,1024]{4,3,2,1,0:T(8,128)(2,1)}), bf16[8,2,2,64,1024]{4,3,2,1,0:T(8,128)(2,1)}, u32[]{:S(2)}, u32[]{:S(2)}) async-start(bf16[8,2,2,64,1024]{4,3,2,1,0:T(8,128)(2,1)} %bitcast.105), calls=%async_computation.1 | async-start | bytes 8388608 | tf_op jit(solution)/shard_map/all_to_all | solution.py:137
  28.5 3.6 %copy-start.28 = (bf16[1,128,1024]{2,1,0:T(8,128)(2,1)S(1)}, bf16[1,128,1024]{2,1,0:T(8,128)(2,1)}, u32[]{:S(2)}) copy-start(bf16[1,128,1024]{2,1,0:T(8,128)(2,1)} %param.14) | copy-start | bytes 786436
  28.6 4.0 %copy-start.25 = (bf16[1,128,1024]{2,1,0:T(8,128)(2,1)S(1)}, bf16[1,128,1024]{2,1,0:T(8,128)(2,1)}, u32[]{:S(2)}) copy-start(bf16[1,128,1024]{2,1,0:T(8,128)(2,1)} %param.18) | copy-start | bytes 786436
  28.6 4.3 %copy-start.29 = (bf16[1,128,1024]{2,1,0:T(8,128)(2,1)S(1)}, bf16[1,128,1024]{2,1,0:T(8,128)(2,1)}, u32[]{:S(2)}) copy-start(bf16[1,128,1024]{2,1,0:T(8,128)(2,1)} %param.17) | copy-start | bytes 786436
  28.6 150.4 %all-reduce.8.cloned.1.call-start = ((), (), s32[]{:S(2)}) async-start(), calls=%async_computation.3 | async-start | bytes 2097152 | tf_op jit(solution)/shard_map/psum | solution.py:109
  29.5 56.1 %collective-permute-start = (bf16[2,64,1024]{2,1,0:T(8,128)(2,1)}, bf16[2,64,1024]{2,1,0:T(8,128)(2,1)}, u32[]{:S(2)}, u32[]{:S(2)}) collective-permute-start(bf16[2,64,1024]{2,1,0:T(8,128)(2,1)} %get-tuple-element.67), channel_id=1, source_target_pairs={{0,1},{1,2},{2,3},{3,4},{4,5},{5,6},{6,7},{7,0},{8,9},{9,10},{10,1... | collective-permute-start | bytes 786440 | tf_op jit(solution)/shard_map/ppermute | solution.py:18
  29.9 55.7 %collective-permute-start.1 = (bf16[2,64,1024]{2,1,0:T(8,128)(2,1)}, bf16[2,64,1024]{2,1,0:T(8,128)(2,1)}, u32[]{:S(2)}, u32[]{:S(2)}) collective-permute-start(bf16[2,64,1024]{2,1,0:T(8,128)(2,1)} %get-tuple-element.68), channel_id=1, source_target_pairs={{1,0},{2,1},{3,2},{4,3},{5,4},{6,5},{7,6},{0,7},{9,8},{10,9},{11,1... | collective-permute-start | bytes 786440 | tf_op jit(solution)/shard_map/ppermute | solution.py:21
  32.9 67.1 %copy-start.2 = (bf16[2,64,16,64]{3,2,1,0:T(8,128)(2,1)}, bf16[2,64,16,64]{3,2,1,0:T(8,128)(2,1)S(1)}, u32[]{:S(2)}) copy-start(bf16[2,64,16,64]{3,2,1,0:T(8,128)(2,1)S(1)} %reshape.259) | copy-start | bytes 786436
  99.6 1.3 copy-start.11
  100.0 1.5 copy-start
  120.5 1.8 copy-start.24
  122.3 1.4 copy-start.4
  122.7 1.3 copy-start.6
  122.7 1.4 copy-start.23
  131.4 3.1 %copy-start.7 = (bf16[2,3,64,16,64]{4,2,3,1,0:T(8,128)(2,1)S(1)}, bf16[2,3,64,16,64]{4,2,3,1,0:T(8,128)(2,1)}, u32[]{:S(2)}) copy-start(bf16[2,3,64,16,64]{4,2,3,1,0:T(8,128)(2,1)} %copy-done.6) | copy-start | bytes 2359300
  135.6 2.2 copy-start.22
  145.4 5.0 %copy-start.13 = (f32[2,192,16,64]{1,3,2,0:T(8,128)S(1)}, f32[2,192,16,64]{1,3,2,0:T(8,128)}, u32[]{:S(2)}) copy-start(f32[2,192,16,64]{1,3,2,0:T(8,128)} %multiply_bitcast_fusion) | copy-start | bytes 4718596
  145.4 75.0 %all-to-all-start.2 = ((bf16[8,2,2,64,1024]{4,3,2,1,0:T(8,128)(2,1)}), bf16[8,2,2,64,1024]{4,3,2,1,0:T(8,128)(2,1)}, u32[]{:S(2)}, u32[]{:S(2)}) async-start(bf16[8,2,2,64,1024]{4,3,2,1,0:T(8,128)(2,1)} %bitcast.104), calls=%async_computation.2 | async-start | bytes 8388608 | tf_op jit(solution)/shard_map/all_to_all | solution.py:153
  153.3 2.9 %copy-start.1 = (f32[2,16,192,64]{2,3,1,0:T(8,128)S(1)}, f32[2,16,192,64]{2,3,1,0:T(8,128)}, u32[]{:S(2)}) copy-start(f32[2,16,192,64]{2,3,1,0:T(8,128)} %copy-done) | copy-start | bytes 4718596
  153.3 2.9 %copy-start.3 = (bf16[2,64,16,64]{3,2,1,0:T(8,128)(2,1)S(1)}, bf16[2,64,16,64]{3,2,1,0:T(8,128)(2,1)}, u32[]{:S(2)}) copy-start(bf16[2,64,16,64]{3,2,1,0:T(8,128)(2,1)} %copy-done.2) | copy-start | bytes 786436
  160.2 2.1 copy-start.21
  162.4 2.2 copy-start.17
  162.4 4.9 %copy-start.12 = (bf16[2,2,192,16,64]{2,4,3,1,0:T(8,128)(2,1)S(1)}, bf16[2,2,192,16,64]{2,4,3,1,0:T(8,128)(2,1)}, u32[]{:S(2)}) copy-start(bf16[2,2,192,16,64]{2,4,3,1,0:T(8,128)(2,1)} %copy-done.11) | copy-start | bytes 4718596
  162.4 4.9 %copy-start.15 = (bf16[2,16,192,64]{2,3,1,0:T(8,128)(2,1)S(1)}, bf16[2,16,192,64]{2,3,1,0:T(8,128)(2,1)}, u32[]{:S(2)}) copy-start(bf16[2,16,192,64]{2,3,1,0:T(8,128)(2,1)} %copy-done.14) | copy-start | bytes 2359300
  164.7 47.5 %collective-permute-start.2 = (f32[2,64,1024]{2,1,0:T(8,128)}, f32[2,64,1024]{2,1,0:T(8,128)}, u32[]{:S(2)}, u32[]{:S(2)}) collective-permute-start(f32[2,64,1024]{2,1,0:T(8,128)} %get-tuple-element.52), channel_id=1, source_target_pairs={{0,1},{1,2},{2,3},{3,4},{4,5},{5,6},{6,7},{7,0},{8,9},{9,10},{10,1... | collective-permute-start | bytes 1572872 | tf_op jit(solution)/shard_map/ppermute | solution.py:18
  164.8 49.4 %collective-permute-start.3 = (f32[2,64,1024]{2,1,0:T(8,128)}, f32[2,64,1024]{2,1,0:T(8,128)}, u32[]{:S(2)}, u32[]{:S(2)}) collective-permute-start(f32[2,64,1024]{2,1,0:T(8,128)} %get-tuple-element.51), channel_id=1, source_target_pairs={{1,0},{2,1},{3,2},{4,3},{5,4},{6,5},{7,6},{0,7},{9,8},{10,9},{11,1... | collective-permute-start | bytes 1572872 | tf_op jit(solution)/shard_map/ppermute | solution.py:21
  182.1 34.3 %copy-start.5 = (bf16[6,1,64,16,64]{4,3,2,1,0:T(8,128)(2,1)S(1)}, bf16[6,1,64,16,64]{4,3,2,1,0:T(8,128)(2,1)}, u32[]{:S(2)}) copy-start(bf16[6,1,64,16,64]{4,3,2,1,0:T(8,128)(2,1)} %copy-done.4) | copy-start | bytes 2359300
  182.1 34.3 %copy-start.9 = (bf16[6,16,64,64]{3,2,1,0:T(8,128)(2,1)S(1)}, bf16[6,16,64,64]{3,2,1,0:T(8,128)(2,1)}, u32[]{:S(2)}) copy-start(bf16[6,16,64,64]{3,2,1,0:T(8,128)(2,1)} %copy-done.8) | copy-start | bytes 2359300
  217.1 1.4 copy-start.20
  (7 other events, 7.2 us)
Sparse Core Ops, SparseCore 0:
  39.0 139.9 all-reduce.7
where the time goes:
time: 248 us; the launch traced here: 247 us
  local copies, waits for them, and re-layouts  84.7 us (34%)
  waiting for transfers between devices  81.6 us (33%)
  other arithmetic  32.2 us (13%)
  starting transfers between devices  20.2 us (8%)
  between operations  14.7 us (6%)
  matrix products  13.6 us (5%)
    ppermute x2, waiting for transfers between devices, extended(): lax.ppermute(lax.slice_in_dim(block, block.shape[dim] - width, None, axis...  67.8 us
    reshape x6, local copies, waits for them, and re-layouts, split_blocks(): return section.reshape(2, blocks, BLK, HEADS, HDIM)  13.2 us
    reshape x1, local copies, waits for them, and re-layouts, shards(): chosen = fetched.reshape(slots_all, 2, BLK, HEADS, HDIM)[slot_index]  11.6 us
    unnamed x68, local copies, waits for them, and re-layouts  11.1 us
    scatter-add x1, other arithmetic, shards(): kv_rand = jnp.zeros((blocks, 2, BLK, feature_dim), jnp.float32).at[asked_...  10.8 us
    psum x1, waiting for transfers between devices, shards(): memory_total = lax.psum(mem_terms, ('dp', 'ctx'))  10.2 us
    convert_element_type x1, other arithmetic, shards(): received.astype(jnp.float32)  6.53 us
    all_to_all x1, starting transfers between devices, shards(): lax.all_to_all(wanted, 'ctx', split_axis=0, concat_axis=0, tiled=True)  5.17 us
  transfers between devices with their start and end apart: 8, of which 4 were waited for; matrix products, arithmetic and copies ran while one was open for 40% of the time, Pallas kernels for 0%

commit v1 on v0

--- a/solution.py
+++ b/solution.py
@@ -106,7 +106,7 @@
     mem_terms = jnp.stack([jnp.sum(dk_mem, axis=0), jnp.sum(dv_mem, axis=0)]).reshape(
         2, GLOB, feature_dim
     )
-    memory_total = lax.psum(mem_terms, ("dp", "ctx"))
+    memory_total = jnp.sum(lax.all_gather(mem_terms, ("dp", "ctx")), axis=0)
     capacity = min(blocks, max(2, 2 * blocks * per_block // cycle_size))
     owner_flat = rand_owner.reshape(-1)
     local_flat = rand_local.reshape(-1)

time: 248 us -> 306 us (1.23)
  waiting for transfers between devices: 81.6 us -> 142 us
  local copies, waits for them, and re-layouts: 84.7 us -> 76.8 us
  other arithmetic: 32.2 us -> 39 us
    ppermute x2, waiting for transfers between devices: 67.8 us -> 138 us  [extended(): lax.ppermute(lax.slice_in_dim(block, block.shape[dim] - width, None, axis...]
    reduce_sum x0 -> x1, other arithmetic: none -> 11.9 us  [shards(): memory_total = jnp.sum(lax.all_gather(mem_terms, ('dp', 'ctx')), axis=0)]
    psum x1 -> x0, waiting for transfers between devices: 10.2 us -> none  [shards(): memory_total = lax.psum(mem_terms, ('dp', 'ctx'))]
    unnamed x68 -> x56, local copies, waits for them, and re-layouts: 11.1 us -> 4.98 us
  transfers between devices with their start and end apart: 8 -> 8, of which waited for: 4 -> 3; matrix products, arithmetic and copies ran while one was open for 40% -> 33% of each run, Pallas kernels for 0% -> 0%
where the time goes in v1:
time: 306 us; the launch traced here: 305 us
  waiting for transfers between devices  142 us (46%)
  local copies, waits for them, and re-layouts  76.8 us (25%)
  other arithmetic  39 us (13%)
  starting transfers between devices  19.9 us (7%)
  between operations  14.8 us (5%)
  matrix products  12 us (4%)
    ppermute x2, waiting for transfers between devices, extended(): lax.ppermute(lax.slice_in_dim(block, block.shape[dim] - width, None, axis...  138 us
    reshape x6, local copies, waits for them, and re-layouts, split_blocks(): return section.reshape(2, blocks, BLK, HEADS, HDIM)  13.1 us
    reshape x1, local copies, waits for them, and re-layouts, shards(): chosen = fetched.reshape(slots_all, 2, BLK, HEADS, HDIM)[slot_index]  11.9 us
    reduce_sum x1, other arithmetic, shards(): memory_total = jnp.sum(lax.all_gather(mem_terms, ('dp', 'ctx')), axis=0)  11.9 us
    scatter-add x1, other arithmetic, shards(): kv_rand = jnp.zeros((blocks, 2, BLK, feature_dim), jnp.float32).at[asked_...  10.8 us
    convert_element_type x1, other arithmetic, shards(): received.astype(jnp.float32)  7.11 us
  transfers between devices with their start and end apart: 8, of which 3 were waited for; matrix products, arithmetic and copies ran while one was open for 33% of the time, Pallas kernels for 0%

profile of v1, /device:TPU:0, one launch (start us, length us, event | category | flops | bytes accessed | tf_op | source)
XLA Modules:
  0.0 304.7 jit_solution(18110211301348074340)
XLA Ops:
  18.8 5.2 %all-to-all-start = ((s32[8,1,2]{2,1,0:T(1,128)}), s32[8,1,2]{2,1,0:T(1,128)S(1)}, u32[]{:S(2)}, u32[]{:S(2)}) async-start(s32[8,1,2]{2,1,0:T(1,128)} %bitcast.12), calls=%async_computation | async-start | bytes 8192 | tf_op jit(solution)/shard_map/all_to_all | solution.py:134
  24.0 4.5 %all-to-all-done = s32[8,1,2]{2,1,0:T(1,128)S(1)} async-done(((s32[8,1,2]{2,1,0:T(1,128)}), s32[8,1,2]{2,1,0:T(1,128)S(1)}, u32[]{:S(2)}, u32[]{:S(2)}) %all-to-all-start) | async-done | bytes 96 | tf_op jit(solution)/shard_map/all_to_all | solution.py:134
  28.8 2.8 gather_fusion
  31.6 4.5 %all-to-all-start.1 = ((bf16[8,2,2,64,1024]{4,3,2,1,0:T(8,128)(2,1)}), bf16[8,2,2,64,1024]{4,3,2,1,0:T(8,128)(2,1)}, u32[]{:S(2)}, u32[]{:S(2)}) async-start(bf16[8,2,2,64,1024]{4,3,2,1,0:T(8,128)(2,1)} %bitcast.107), calls=%async_computation.1 | async-start | bytes 8388608 | tf_op jit(solution)/shard_map/all_to_all | solution.py:137
  36.7 2.3 collective-permute-start.1
  38.9 1.6 reshape.254
  42.4 2.0 copy.162
  45.7 71.5 %collective-permute-done = bf16[2,64,1024]{2,1,0:T(8,128)(2,1)} collective-permute-done((bf16[2,64,1024]{2,1,0:T(8,128)(2,1)S(1)}, bf16[2,64,1024]{2,1,0:T(8,128)(2,1)}, u32[]{:S(2)}, u32[]{:S(2)}) %collective-permute-start) | collective-permute-done | bytes 262176 | tf_op jit(solution)/shard_map/ppermute | solution.py:18
  117.2 1.9 pad_maximum_fusion.4
  119.2 2.5 reshape.253
  121.6 2.7 copy.161
  124.3 1.6 reshape.255
  126.0 2.7 copy.163
  128.6 2.5 pad_maximum_fusion
  134.2 1.8 multiply_bitcast_fusion
  136.0 11.9 %reshape.261 = bf16[16,2,64,16,64]{4,3,2,1,0:T(8,128)(2,1)} reshape(bf16[8,2,2,64,1024]{4,3,2,1,0:T(8,128)(2,1)} %all-to-all-done.1) | data formatting | bytes 8388608 | tf_op jit(solution)/shard_map/reshape | solution.py:140
  147.9 4.8 %gather_fusion.1 = bf16[6,2,64,16,64]{4,3,2,1,0:T(8,128)(2,1)S(1)} fusion(bf16[16,2,64,16,64]{4,3,2,1,0:T(8,128)(2,1)} %reshape.261, s32[1024]{0:T(1024)S(1)} %pad_clamp_fusion), kind=kCustom, calls=%fused_computation.1 | custom fusion | bytes 3145752 | tf_op jit(solution)/shard_map/gather | solution.py:140
  157.9 2.2 copy.188
  160.1 3.5 %stack.38 = bf16[6,1,64,1024]{3,2,0,1:T(8,128)(2,1)} reshape(bf16[6,64,16,64]{3,2,1,0:T(8,128)(2,1)} %copy.188) | data formatting | bytes 1572864 | tf_op jit(solution)/shard_map/stack | solution.py:146
  163.6 2.1 fusion.5
  168.2 2.5 broadcast_in_dim.51
  170.7 4.8 %scatter_fusion = bf16[16,2,64,1024]{3,2,1,0:T(8,128)(2,1)} fusion(bf16[16,2,64,1024]{3,2,1,0:T(8,128)(2,1)} %broadcast_in_dim.51, s32[6]{0:T(128)S(1)} %fusion.34, bf16[6,2,64,1024]{3,2,1,0:T(8,128)(2,1)S(1)} %copy.190), kind=kCustom, calls=%fused_computation.3 | custom fusion | bytes 4718616 | tf_op jit(solution)/shard_map/scatter | solution.py:151
  175.5 4.7 %all-to-all-start.2 = ((bf16[8,2,2,64,1024]{4,3,2,1,0:T(8,128)(2,1)}), bf16[8,2,2,64,1024]{4,3,2,1,0:T(8,128)(2,1)}, u32[]{:S(2)}, u32[]{:S(2)}) async-start(bf16[8,2,2,64,1024]{4,3,2,1,0:T(8,128)(2,1)} %bitcast.106), calls=%async_computation.2 | async-start | bytes 8388608 | tf_op jit(solution)/shard_map/all_to_all | solution.py:153
  181.2 2.0 copy.185
  183.2 2.9 stack.35
  188.0 2.0 copy.187
  190.0 2.1 stack.36
  193.0 2.3 collective-permute-start.3
  195.7 66.2 %collective-permute-done.2 = f32[2,64,1024]{2,1,0:T(8,128)S(1)} collective-permute-done((f32[2,64,1024]{2,1,0:T(8,128)S(1)}, f32[2,64,1024]{2,1,0:T(8,128)S(1)}, u32[]{:S(2)}, u32[]{:S(2)}) %collective-permute-start.2) | collective-permute-done | bytes 524320 | tf_op jit(solution)/shard_map/ppermute | solution.py:18
  265.9 7.1 %bitcast_convert_fusion = f32[16,2,64,1024]{3,2,1,0:T(8,128)} fusion(bf16[8,2,2,64,1024]{4,3,2,1,0:T(8,128)(2,1)} %all-to-all-done.2), kind=kLoop, calls=%fused_computation.5 | loop fusion | flops 2097152 | bytes 12582912 | tf_op jit(solution)/shard_map/convert_element_type | solution.py:164
  273.2 10.8 %scatter_fusion.1 = f32[2,2,64,1024]{3,2,1,0:T(8,128)S(1)} fusion(f32[2,2,64,1024]{3,2,1,0:T(8,128)S(1)} %broadcast_in_dim.50, s32[16]{0:T(128)S(1)} %fusion.35, f32[16,2,64,1024]{3,2,1,0:T(8,128)} %bitcast_convert_fusion), kind=kCustom, calls=%fused_computation.4 | custom fusion | flops 2097152 | bytes 25165888 | tf_op jit(solution)/shard_map/scatter-add | solution.py:164
  285.0 11.9 %reduce_sum.62 = f32[2,128,1024]{2,1,0:T(8,128)S(1)} reduce(f32[32,2,128,1024]{3,2,1,0:T(8,128)} %all-gather.2.cloned.1.call-done, f32[]{:T(128)} %constant.77.clone.1), dimensions={0}, to_apply=%region_8.9 | reduce | flops 8126464 | bytes 34603012 | tf_op jit(solution)/shard_map/reduce_sum | solution.py:109
  (138 shorter events, 36.0 us)
Async XLA Ops:
  7.2 277.8 %all-gather.2.cloned.1.call-start = ((), (), s32[]{:S(2)}) async-start(), calls=%async_computation.3 | async-start | bytes 34603008 | tf_op jit(solution)/shard_map/all_gather | solution.py:109
  9.9 121.7 %copy-start.2 = (bf16[2,64,16,64]{3,2,1,0:T(8,128)(2,1)}, bf16[2,64,16,64]{3,2,1,0:T(8,128)(2,1)S(1)}, u32[]{:S(2)}) copy-start(bf16[2,64,16,64]{3,2,1,0:T(8,128)(2,1)S(1)} %reshape.258) | copy-start | bytes 786436
  9.9 2.7 copy-start.22
  10.8 2.0 copy-start.23
  15.5 1.4 copy-start.24
  15.6 1.6 copy-start.25
  15.6 8.4 %copy-start.20 = (bf16[1,128,1024]{2,1,0:T(8,128)(2,1)S(1)}, bf16[1,128,1024]{2,1,0:T(8,128)(2,1)}, u32[]{:S(2)}) copy-start(bf16[1,128,1024]{2,1,0:T(8,128)(2,1)} %param.15) | copy-start | bytes 786436
  15.6 8.4 %copy-start.21 = (bf16[1,128,1024]{2,1,0:T(8,128)(2,1)S(1)}, bf16[1,128,1024]{2,1,0:T(8,128)(2,1)}, u32[]{:S(2)}) copy-start(bf16[1,128,1024]{2,1,0:T(8,128)(2,1)} %param.16) | copy-start | bytes 786436
  18.8 9.8 %all-to-all-start = ((s32[8,1,2]{2,1,0:T(1,128)}), s32[8,1,2]{2,1,0:T(1,128)S(1)}, u32[]{:S(2)}, u32[]{:S(2)}) async-start(s32[8,1,2]{2,1,0:T(1,128)} %bitcast.12), calls=%async_computation | async-start | bytes 8192 | tf_op jit(solution)/shard_map/all_to_all | solution.py:134
  31.6 104.4 %all-to-all-start.1 = ((bf16[8,2,2,64,1024]{4,3,2,1,0:T(8,128)(2,1)}), bf16[8,2,2,64,1024]{4,3,2,1,0:T(8,128)(2,1)}, u32[]{:S(2)}, u32[]{:S(2)}) async-start(bf16[8,2,2,64,1024]{4,3,2,1,0:T(8,128)(2,1)} %bitcast.107), calls=%async_computation.1 | async-start | bytes 8388608 | tf_op jit(solution)/shard_map/all_to_all | solution.py:137
  36.2 81.0 %collective-permute-start = (bf16[2,64,1024]{2,1,0:T(8,128)(2,1)S(1)}, bf16[2,64,1024]{2,1,0:T(8,128)(2,1)}, u32[]{:S(2)}, u32[]{:S(2)}) collective-permute-start(bf16[2,64,1024]{2,1,0:T(8,128)(2,1)S(1)} %get-tuple-element.62), channel_id=1, source_target_pairs={{0,1},{1,2},{2,3},{3,4},{4,5},{5,6},{6,7},{7,0},{8,9},{9,10},{10,1... | collective-permute-start | bytes 786440 | tf_op jit(solution)/shard_map/ppermute | solution.py:18
  36.7 80.6 %collective-permute-start.1 = (bf16[2,64,1024]{2,1,0:T(8,128)(2,1)S(1)}, bf16[2,64,1024]{2,1,0:T(8,128)(2,1)}, u32[]{:S(2)}, u32[]{:S(2)}) collective-permute-start(bf16[2,64,1024]{2,1,0:T(8,128)(2,1)S(1)} %get-tuple-element.63), channel_id=1, source_target_pairs={{1,0},{2,1},{3,2},{4,3},{5,4},{6,5},{7,6},{0,7},{9,8},{10,9},{11,1... | collective-permute-start | bytes 786440 | tf_op jit(solution)/shard_map/ppermute | solution.py:21
  131.2 1.4 copy-start.9
  131.6 1.6 copy-start
  152.7 1.0 copy-start.19
  153.3 1.8 copy-start.4
  154.1 1.0 copy-start.18
  155.6 1.2 copy-start.8
  156.7 1.2 copy-start.6
  165.7 2.2 copy-start.17
  175.5 4.8 %copy-start.11 = (f32[2,192,16,64]{1,3,2,0:T(8,128)S(1)}, f32[2,192,16,64]{1,3,2,0:T(8,128)}, u32[]{:S(2)}) copy-start(f32[2,192,16,64]{1,3,2,0:T(8,128)} %multiply_bitcast_fusion) | copy-start | bytes 4718596
  175.5 90.4 %all-to-all-start.2 = ((bf16[8,2,2,64,1024]{4,3,2,1,0:T(8,128)(2,1)}), bf16[8,2,2,64,1024]{4,3,2,1,0:T(8,128)(2,1)}, u32[]{:S(2)}, u32[]{:S(2)}) async-start(bf16[8,2,2,64,1024]{4,3,2,1,0:T(8,128)(2,1)} %bitcast.106), calls=%async_computation.2 | async-start | bytes 8388608 | tf_op jit(solution)/shard_map/all_to_all | solution.py:153
  183.2 2.9 copy-start.1
  183.2 2.9 copy-start.3
  190.0 2.1 copy-start.16
  192.3 3.0 copy-start.10
  192.3 3.0 copy-start.13
  192.4 69.5 %collective-permute-start.2 = (f32[2,64,1024]{2,1,0:T(8,128)S(1)}, f32[2,64,1024]{2,1,0:T(8,128)S(1)}, u32[]{:S(2)}, u32[]{:S(2)}) collective-permute-start(f32[2,64,1024]{2,1,0:T(8,128)S(1)} %get-tuple-element.47), channel_id=1, source_target_pairs={{0,1},{1,2},{2,3},{3,4},{4,5},{5,6},{6,7},{7,0},{8,9},{9,10},{10,1... | collective-permute-start | bytes 1572872 | tf_op jit(solution)/shard_map/ppermute | solution.py:18
  193.0 69.0 %collective-permute-start.3 = (f32[2,64,1024]{2,1,0:T(8,128)S(1)}, f32[2,64,1024]{2,1,0:T(8,128)S(1)}, u32[]{:S(2)}, u32[]{:S(2)}) collective-permute-start(f32[2,64,1024]{2,1,0:T(8,128)S(1)} %get-tuple-element.46), channel_id=1, source_target_pairs={{1,0},{2,1},{3,2},{4,3},{5,4},{6,5},{7,6},{0,7},{9,8},{10,9},{11,1... | collective-permute-start | bytes 1572872 | tf_op jit(solution)/shard_map/ppermute | solution.py:21
  195.7 66.5 %copy-start.5 = (bf16[6,1,64,16,64]{4,3,2,1,0:T(8,128)(2,1)S(1)}, bf16[6,1,64,16,64]{4,3,2,1,0:T(8,128)(2,1)}, u32[]{:S(2)}) copy-start(bf16[6,1,64,16,64]{4,3,2,1,0:T(8,128)(2,1)} %copy-done.4) | copy-start | bytes 2359300
  195.7 66.5 %copy-start.7 = (bf16[6,16,64,64]{3,2,1,0:T(8,128)(2,1)S(1)}, bf16[6,16,64,64]{3,2,1,0:T(8,128)(2,1)}, u32[]{:S(2)}) copy-start(bf16[6,16,64,64]{3,2,1,0:T(8,128)(2,1)} %copy-done.6) | copy-start | bytes 2359300
  263.0 1.0 copy-start.15
  (2 other events, 1.8 us)
Sparse Core Ops, SparseCore 0:
  17.1 257.4 all-gather.1
